TPU v7x, 32 devices: a whole 2x2x4 slice. The times are simulated.
32 devices in a mesh: rep: 2 (over x), group: 4 (over z), proto: 4 (over y, core).
Axes of the slice: x: 2, y: 2, z: 4, core: 2. Of those that a mesh axis runs over, the one named last changes fastest.
Arguments:
- embeddings: bfloat16 [16384, 768], P(('rep', 'group')), may hold values from -6 to 6
- labels: int32 [16384], P(('rep', 'group')), may hold values from 0 to 255, as said below
- cluster_place: int32 [256], replicated, may hold values from 0 to 255, as said below
- row_counts: int32 [8], P(('rep', 'group')), may hold values from 1536 to 2048, as said below
- prototypes: bfloat16 [256, 64, 768], P('group', 'proto'), may hold values from -6 to 6
Outputs:
- new_prototypes: float32 [256, 64, 768], P('group', 'proto', 'rep')
- codes: float32 [16384, 64], P(('rep', 'group'), 'proto')
Inputs may be any that keep to these rules, and one draw needn't show every extreme that they name: Among the live rows of one block of 2048 rows, at most 1024 have labels whose place lies in any one group (place // 64); in every draw some group gets exactly 1024 live rows from every block. `cluster_place`: A permutation of the coarse clusters. `row_counts`: rows of a block at positions of its count and beyond are padding.
All inputs are finite; a program needn't handle non-finite values.
Results may differ from a plain program's by a relative error of at most 0.0042.
Values may be sent and summed in bfloat16 or wider, within the bound.
A program may use at most 128 MiB of HBM per device.

v0:
```python
import jax
import jax.numpy as jnp
from jax import lax
from jax.sharding import PartitionSpec as P

FPC = 64
ITERS = 3


sharpness_divisor = 0.03


def unit(values):
    return values * lax.rsqrt(jnp.mean(values * values, axis=-1, keepdims=True) + 1e-06)


def grouped_moment(left, right, group_sizes):
    numbers = lax.RaggedDotDimensionNumbers(
        dot_dimension_numbers=(((0,), (0,)), ((), ())),
        lhs_ragged_dimensions=[0],
        rhs_group_dimensions=[],
    )
    return lax.ragged_dot_general(
        left, right, group_sizes, numbers, preferred_element_type=jnp.float32
    )


def body(embeddings, labels, cluster_place, row_counts, prototypes):
    rows_here = embeddings.shape[0]
    image_vectors = embeddings.shape[1]
    groups = lax.axis_size("group")
    replicas = lax.axis_size("rep")
    capacity = rows_here // max(groups // 4, 2)
    clusters = prototypes.shape[0]
    fine_local = prototypes.shape[1]
    unit_rows = unit(embeddings.astype(jnp.float32)).astype(jnp.bfloat16)
    sample_location = jnp.take(cluster_place, labels)
    target = sample_location // clusters
    slot_row = sample_location % clusters
    live_send = jnp.arange(rows_here) < row_counts[0]
    choose = (target[:, None] == jnp.arange(groups)[None, :]) & live_send[:, None]
    running = jnp.cumsum(choose.astype(jnp.int32), axis=0) - 1
    position = jnp.sum(jnp.where(choose, running, 0), axis=1)
    bucket = jnp.where(live_send, target, groups)
    send_rows = (
        jnp.zeros((groups, capacity, image_vectors), jnp.bfloat16)
        .at[bucket, position]
        .set(unit_rows, mode="drop")
    )
    send_slots = (
        jnp.zeros((groups, capacity), jnp.int32).at[bucket, position].set(slot_row + 1, mode="drop")
    )
    got_rows, got_slots = (
        lax.all_to_all(send_rows, "group", split_axis=0, concat_axis=0, tiled=True),
        lax.all_to_all(send_slots, "group", split_axis=0, concat_axis=0, tiled=True),
    )
    received = groups * capacity
    arrived = got_rows.reshape(received, image_vectors)
    arrived_slot = got_slots.reshape(received) - 1
    arrived_live = arrived_slot >= 0
    sort_key = jnp.where(arrived_live, arrived_slot, clusters).astype(jnp.int32)
    order = jnp.argsort(sort_key, stable=True)
    sorted_rows = jnp.take(arrived, order, axis=0)
    sorted_slot = jnp.take(sort_key, order)
    active_sorted_rows = sorted_slot < clusters
    member = sorted_slot[:, None] == jnp.arange(clusters)[None, :]
    member_f = member.astype(jnp.float32)
    group_sizes = jnp.sum(member.astype(jnp.int32), axis=0)
    proto_f = prototypes.astype(jnp.float32)
    columns_all = clusters * fine_local
    proto_cols = jnp.swapaxes(unit(proto_f).astype(jnp.bfloat16), 1, 2)
    chosen_samples = lax.ragged_dot(
        sorted_rows, proto_cols, group_sizes, preferred_element_type=jnp.float32
    )
    balanced_transport_routine = jnp.where(
        active_sorted_rows[:, None],
        jnp.exp(chosen_samples * (1.0 / (image_vectors * sharpness_divisor))),
        0.0,
    )

    def column_part(sample_importance):
        return lax.dot_general(
            member_f,
            balanced_transport_routine * sample_importance[:, None],
            (((0,), (0,)), ((), ())),
            precision=lax.Precision.HIGHEST,
        )

    sample_importance = active_sorted_rows.astype(jnp.float32)
    count_local = jnp.sum(member_f, axis=0)
    column_sum, counts = lax.psum((column_part(sample_importance), count_local), "rep")
    occupied = counts[:, None] > 0
    sample_wise = jnp.zeros_like(balanced_transport_routine)
    for iteration in range(ITERS):
        if iteration > 0:
            column_sum = lax.psum(column_part(sample_importance), "rep")
        normalizer_factor = jnp.where(
            occupied, counts[:, None] / FPC / jnp.where(occupied, column_sum, 1.0), 0.0
        )
        sample_wise = jnp.dot(member_f, normalizer_factor, precision=lax.Precision.HIGHEST)
        sample_total = lax.psum(jnp.sum(balanced_transport_routine * sample_wise, axis=1), "proto")
        sample_importance = jnp.where(
            active_sorted_rows, 1.0 / jnp.where(active_sorted_rows, sample_total, 1.0), 0.0
        )
    transport_piece = sample_importance[:, None] * balanced_transport_routine * sample_wise
    mass_local = lax.dot_general(
        member_f, transport_piece, (((0,), (0,)), ((), ())), precision=lax.Precision.HIGHEST
    ).reshape(columns_all)
    plan_low = transport_piece.astype(jnp.bfloat16)
    previous = proto_f.reshape(columns_all, image_vectors)
    half_width = image_vectors // replicas
    moment = grouped_moment(plan_low, sorted_rows, group_sizes).reshape(columns_all, image_vectors)
    moment, col_mass = lax.psum((moment, mass_local), "rep")
    updated = (previous + moment) / (1.0 + col_mass[:, None])
    renewed = unit(updated)
    renewed = lax.dynamic_slice_in_dim(renewed, lax.axis_index("rep") * half_width, half_width, 1)
    new_prototypes = renewed.reshape(clusters, fine_local, half_width)
    plan_slots = jnp.zeros_like(transport_piece).at[order].set(transport_piece)
    returned = lax.all_to_all(
        (FPC * plan_slots).reshape(groups, capacity, fine_local),
        "group",
        split_axis=0,
        concat_axis=0,
        tiled=True,
    )
    code_rows = jnp.where(
        live_send[:, None], returned[jnp.where(live_send, target, 0), position], 0.0
    )
    return (new_prototypes, code_rows)


def solution(mesh):
    return jax.shard_map(
        body,
        mesh=mesh,
        in_specs=(
            P(("rep", "group"), None),
            P(("rep", "group")),
            P(),
            P(("rep", "group")),
            P("group", "proto", None),
        ),
        out_specs=(P("group", "proto", "rep"), P(("rep", "group"), "proto")),
        check_vma=False,
    )
```

profile of v0, /device:TPU:0, one launch (start us, length us, event | category | flops | bytes accessed | tf_op | source)
XLA Modules:
  0.0 487.1 jit_solution(10842648182470674715)
XLA Ops:
  8.6 13.2 %gather_fusion = s32[2048]{0:T(1024)S(1)} fusion(s32[256]{0:T(256)S(1)} %copy-done, s32[2048]{0:T(1024)S(1)} %fusion.53), kind=kCustom, calls=%fused_computation | custom fusion | bytes 24576 | tf_op jit(solution)/shard_map/jit(_take)/gather | solution.py:37
  23.9 8.6 %scatter_custom_fusion.1 = s32[4096]{0:T(1024)} fusion(s32[2048]{0:T(1024)S(1)} %broadcast_select_fusion.3, s32[2048]{0:T(1024)S(1)} %get-tuple-element.36, s32[]{:T(128)} %constant.57.clone.1), kind=kCustom, calls=%fused_computation.88 | custom fusion | bytes 16388
  32.5 6.3 %all-to-all-start = ((s32[4,1,1024]{2,1,0:T(1,128)}), s32[4,1,1024]{2,1,0:T(1,128)S(1)}, u32[]{:S(2)}, u32[]{:S(2)}) async-start(s32[4,1,1024]{2,1,0:T(1,128)} %bitcast.6), calls=%async_computation | async-start | bytes 32768 | tf_op jit(solution)/shard_map/all_to_all | solution.py:55
  39.5 14.2 %scatter_custom_fusion.2 = bf16[4096,768]{1,0:T(8,128)(2,1)} fusion(s32[2048]{0:T(1024)S(1)} %broadcast_select_fusion.3, bf16[2048,768]{1,0:T(8,128)(2,1)S(1)} %copy-done.5, bf16[]{:T(256)} %constant.117.clone.1, f32[2048]{0:T(1024)S(1)} %add_rsqrt_fusion.1), kind=kCustom, calls=%fused_computation.14 | custom fusion | flops 4718592 | bytes 9445378
  53.7 5.4 %all-to-all-start.1 = ((bf16[4,1024,768]{2,1,0:T(8,128)(2,1)}), bf16[4,1024,768]{2,1,0:T(8,128)(2,1)}, u32[]{:S(2)}, u32[]{:S(2)}) async-start(bf16[4,1024,768]{2,1,0:T(8,128)(2,1)} %bitcast.41), calls=%async_computation.1 | async-start | bytes 12582912 | tf_op jit(solution)/shard_map/all_to_all | solution.py:54
  60.1 8.4 %copy.38 = bf16[64,16,768]{1,2,0:T(8,128)(2,1)} copy(bf16[64,16,768]{2,1,0:T(8,128)(2,1)S(1)} %multiply_convert_fusion) | data formatting | bytes 3145728 | tf_op jit(solution)/shard_map/convert_element_type | solution.py:71
  68.5 5.8 %sort.17 = (s32[4096]{0:T(1024)}, s32[4096]{0:T(1024)S(1)}) sort(s32[4096]{0:T(1024)S(1)} %compare_select_fusion.2, s32[4096]{0:T(1024)S(1)} %iota.43), dimensions={0}, to_apply=%region_4.5 | sort | flops 49152 | bytes 65536 | tf_op jit(solution)/shard_map/jit(argsort)/sort | solution.py:62
  74.3 23.0 %gather_fusion.1 = s32[4096]{0:T(1024)S(1)} fusion(s32[4096]{0:T(1024)S(1)} %compare_select_fusion.2, s32[4096]{0:T(1024)S(1)} %get-tuple-element.35), kind=kCustom, calls=%fused_computation.1 | custom fusion | bytes 49152 | tf_op jit(solution)/shard_map/jit(_take)/gather | solution.py:64
  98.0 3.6 ragged-dot-metadata.1
  101.6 3.7 ragged-dot-metadata
  105.5 91.8 %all-to-all-done.1 = bf16[4,1024,768]{2,1,0:T(8,128)(2,1)} async-done(((bf16[4,1024,768]{2,1,0:T(8,128)(2,1)}), bf16[4,1024,768]{2,1,0:T(8,128)(2,1)}, u32[]{:S(2)}, u32[]{:S(2)}) %all-to-all-start.1) | async-done | bytes 6291488 | tf_op jit(solution)/shard_map/all_to_all | solution.py:54
  197.3 22.7 %gather_fusion.2 = bf16[4096,768]{1,0:T(8,128)(2,1)} fusion(bf16[4096,768]{1,0:T(8,128)(2,1)} %bitcast.9, s32[4096]{0:T(1024)S(1)} %get-tuple-element.35), kind=kCustom, calls=%fused_computation.2 | custom fusion | bytes 12599296 | tf_op jit(solution)/shard_map/jit(_take)/gather | solution.py:63
  219.9 7.5 %broadcast_select_fusion = bf16[4096,768]{1,0:T(8,128)(2,1)} fusion(bf16[4096,768]{1,0:T(8,128)(2,1)} %gather_fusion.2, pred[4096]{0:T(1024)(128)(4,1)S(1)} %get-tuple-element.33), kind=kLoop, calls=%fused_computation.11 | loop fusion | flops 3145728 | bytes 12587008 | tf_op jit(solution)/shard_map/jit(_take)/select_n | solution.py:63
  227.4 45.2 %ragged-dot-none.1 = f32[4096,16]{1,0:T(8,128)} custom-call(s32[1]{0:T(128)} %get-tuple-element.8, s32[65]{0:T(128)} %get-tuple-element.9, s32[79]{0:T(128)} %get-tuple-element.10, s32[79]{0:T(128)} %get-tuple-element.11, s32[1]{0:T(128)} %get-tuple-element.8, bf16[4096,768]{1,0:T(8,128)(2,1)} %broadcast_select_fusion, bf16[64,768,16]{2,1,0:T(8,128)(2,1)} %bitcast.40), custom_call_target="tpu_custom_call" | custom-call | flops 100663296 | bytes 8126720 | tf_op jit(solution)/shard_map/ragged_dot_general/ragged-dot-none
  272.6 4.8 fusion.11
  277.4 5.0 %all-reduce = (f32[64,16]{0,1:T(8,128)S(1)}, f32[64]{0:T(128)S(1)}) all-reduce(f32[64,16]{0,1:T(8,128)S(1)} %fusion.11, f32[64]{0:T(128)S(1)} %convert_reduce_fusion), channel_id=1, replica_groups=mesh['rep'=2,'group'=4,'proto'=4] {'rep'}, use_global_device_ids=true, to_apply=%region_11.12 | all-reduce | flops 1088 | bytes 8704 | tf_op jit(solution)/shard_map/psum | solution.py:91
  284.8 10.1 %psum.65 = f32[4096]{0:T(1024)S(1)} all-reduce(f32[4096]{0:T(1024)S(1)} %fusion.13), channel_id=1, replica_groups=mesh['rep'=2,'group'=4,'proto'=4] {'proto'}, use_global_device_ids=true, to_apply=%region_13.14 | all-reduce | flops 4096 | bytes 32768 | tf_op jit(solution)/shard_map/psum | solution.py:101
  294.9 2.9 fusion.9
  297.8 5.0 %psum.66 = f32[64,16]{0,1:T(8,128)S(1)} all-reduce(f32[64,16]{0,1:T(8,128)S(1)} %fusion.9), channel_id=1, replica_groups=mesh['rep'=2,'group'=4,'proto'=4] {'rep'}, use_global_device_ids=true, to_apply=%region_14.15 | all-reduce | flops 1024 | bytes 8192 | tf_op jit(solution)/shard_map/psum | solution.py:96
  305.1 10.3 %psum.67 = f32[4096]{0:T(1024)S(1)} all-reduce(f32[4096]{0:T(1024)S(1)} %fusion.14), channel_id=1, replica_groups=mesh['rep'=2,'group'=4,'proto'=4] {'proto'}, use_global_device_ids=true, to_apply=%region_16.17 | all-reduce | flops 4096 | bytes 32768 | tf_op jit(solution)/shard_map/psum | solution.py:101
  315.4 2.9 fusion.7
  318.4 5.0 %psum.68 = f32[64,16]{0,1:T(8,128)S(1)} all-reduce(f32[64,16]{0,1:T(8,128)S(1)} %fusion.7), channel_id=1, replica_groups=mesh['rep'=2,'group'=4,'proto'=4] {'rep'}, use_global_device_ids=true, to_apply=%region_17.18 | all-reduce | flops 1024 | bytes 8192 | tf_op jit(solution)/shard_map/psum | solution.py:96
  323.3 3.4 multiply_reduce_fusion.2
  326.7 10.1 %psum.69 = f32[4096]{0:T(1024)S(1)} all-reduce(f32[4096]{0:T(1024)S(1)} %get-tuple-element.39), channel_id=1, replica_groups=mesh['rep'=2,'group'=4,'proto'=4] {'proto'}, use_global_device_ids=true, to_apply=%region_19.20 | all-reduce | flops 4096 | bytes 32768 | tf_op jit(solution)/shard_map/psum | solution.py:101
  336.8 4.6 fusion.74
  341.4 34.1 %ragged-dot-none = f32[64,16,768]{2,1,0:T(8,128)} custom-call(s32[1]{0:T(128)} %get-tuple-element.4, s32[65]{0:T(128)} %get-tuple-element.5, s32[79]{0:T(128)} %get-tuple-element.6, s32[79]{0:T(128)} %get-tuple-element.7, s32[1]{0:T(128)} %get-tuple-element.4, bf16[4096,16]{1,0:T(8,128)(2,1)} %get-tuple-element.28, bf16[4096,768]{1,0:T(8,128)(2,1)} %broadcast_select_fusion), custom_call_target="tpu_custom_call" | custom-call | flops 100663296 | bytes 9568512 | tf_op jit(solution)/shard_map/ragged_dot_general/ragged-dot-none
  377.0 12.0 %scatter_custom_fusion = f32[4096,16]{1,0:T(8,128)} fusion(s32[4096]{0:T(1024)S(1)} %get-tuple-element.34, f32[4096,16]{1,0:T(8,128)S(1)} %copy-done.6, f32[]{:T(128)} %constant.118.clone.1), kind=kCustom, calls=%fused_computation.39 | custom fusion | bytes 262148 | tf_op jit(solution)/shard_map/scatter | solution.py:118
  389.1 3.1 broadcast_multiply_fusion
  395.0 18.8 %all-to-all-start.2 = ((f32[4,1024,16]{1,2,0:T(8,128)}), f32[4,1024,16]{1,2,0:T(8,128)S(1)}, u32[]{:S(2)}, u32[]{:S(2)}) async-start(f32[4,1024,16]{1,2,0:T(8,128)} %copy.44), calls=%async_computation.2 | async-start | bytes 524288 | tf_op jit(solution)/shard_map/all_to_all | solution.py:119
  414.9 5.1 %psum.71 = f32[1024]{0:T(1024)S(1)} all-reduce(f32[1024]{0:T(1024)S(1)} %reshape.156), channel_id=1, replica_groups=mesh['rep'=2,'group'=4,'proto'=4] {'rep'}, use_global_device_ids=true, to_apply=%region_21.22 | all-reduce | flops 1024 | bytes 8192 | tf_op jit(solution)/shard_map/psum | solution.py:113
  422.9 13.0 %gather_fusion.3 = f32[2048,16]{1,0:T(8,128)S(1)} fusion(f32[4,1024,16]{2,1,0:T(8,128)S(1)} %copy.45, s32[2048]{0:T(1024)S(1)} %bitcast.39), kind=kCustom, calls=%fused_computation.3 | custom fusion | bytes 278528 | tf_op jit(solution)/shard_map/gather | solution.py:127
  439.5 36.8 %all-reduce.3.cloned.1.call-done = f32[1024,768]{1,0:T(8,128)} async-done(((f32[1024,768]{1,0:T(8,128)}), f32[1024,768]{1,0:T(8,128)}) %all-reduce.3.cloned.1.call-update) | async-done | bytes 3145744 | tf_op jit(solution)/shard_map/psum | solution.py:113
  (68 shorter events, 25.9 us)
Async XLA Ops:
  7.2 1.4 copy-start
  8.6 13.3 %copy-start.7 = (s32[2048]{0:T(1024)S(1)}, s32[2048]{0:T(1024)}, u32[]{:S(2)}) copy-start(s32[2048]{0:T(1024)} %param.6) | copy-start | bytes 24580
  8.6 15.1 %copy-start.9 = (s32[2]{0:T(128)S(1)}, s32[2]{0:T(128)}, u32[]{:S(2)}) copy-start(s32[2]{0:T(128)} %constant.130) | copy-start | bytes 28
  8.6 15.1 %copy-start.8 = (s32[2]{0:T(128)S(1)}, s32[2]{0:T(128)}, u32[]{:S(2)}) copy-start(s32[2]{0:T(128)} %constant.133) | copy-start | bytes 28
  8.6 30.2 %copy-start.5 = (bf16[2048,768]{1,0:T(8,128)(2,1)S(1)}, bf16[2048,768]{1,0:T(8,128)(2,1)}, u32[]{:S(2)}) copy-start(bf16[2048,768]{1,0:T(8,128)(2,1)} %param.5) | copy-start | bytes 9437188
  32.5 21.2 %all-to-all-start = ((s32[4,1,1024]{2,1,0:T(1,128)}), s32[4,1,1024]{2,1,0:T(1,128)S(1)}, u32[]{:S(2)}, u32[]{:S(2)}) async-start(s32[4,1,1024]{2,1,0:T(1,128)} %bitcast.6), calls=%async_computation | async-start | bytes 32768 | tf_op jit(solution)/shard_map/all_to_all | solution.py:55
  53.7 5.7 %copy-start.3 = (bf16[64,16,768]{2,1,0:T(8,128)(2,1)S(1)}, bf16[64,16,768]{2,1,0:T(8,128)(2,1)}, u32[]{:S(2)}) copy-start(bf16[64,16,768]{2,1,0:T(8,128)(2,1)} %param.9) | copy-start | bytes 4718596
  53.7 143.6 %all-to-all-start.1 = ((bf16[4,1024,768]{2,1,0:T(8,128)(2,1)}), bf16[4,1024,768]{2,1,0:T(8,128)(2,1)}, u32[]{:S(2)}, u32[]{:S(2)}) async-start(bf16[4,1024,768]{2,1,0:T(8,128)(2,1)} %bitcast.41), calls=%async_computation.1 | async-start | bytes 12582912 | tf_op jit(solution)/shard_map/all_to_all | solution.py:54
  59.1 417.2 %all-reduce.3.cloned.1.call-start = ((), (), s32[]{:S(2)}) async-start(), calls=%async_computation.3 | async-start | bytes 6291456 | tf_op jit(solution)/shard_map/psum | solution.py:113
  272.6 9.9 %copy-start.2 = (f32[4096,16]{1,0:T(8,128)S(1)}, f32[4096,16]{1,0:T(8,128)}, u32[]{:S(2)}) copy-start(f32[4096,16]{1,0:T(8,128)} %ragged-dot-none.1) | copy-start | bytes 786436
  375.5 1.6 copy-start.6
  395.0 27.3 %all-to-all-start.2 = ((f32[4,1024,16]{1,2,0:T(8,128)}), f32[4,1024,16]{1,2,0:T(8,128)S(1)}, u32[]{:S(2)}, u32[]{:S(2)}) async-start(f32[4,1024,16]{1,2,0:T(8,128)} %copy.44), calls=%async_computation.2 | async-start | bytes 524288 | tf_op jit(solution)/shard_map/all_to_all | solution.py:119
  435.9 40.4 %copy-start.4 = (bf16[64,16,768]{2,1,0:T(8,128)(2,1)S(1)}, bf16[64,16,768]{2,1,0:T(8,128)(2,1)}, u32[]{:S(2)}) copy-start(bf16[64,16,768]{2,1,0:T(8,128)(2,1)} %param.9) | copy-start | bytes 4718596
  476.3 4.0 copy-start.1
Sparse Core Ops, SparseCore 0:
  375.6 100.6 all-reduce.2
where the time goes:
time: 490 us; the launch traced here: 487 us
  waiting for transfers between devices  131 us (27%)
  local copies, waits for them, and re-layouts  109 us (22%)
  Pallas kernels  86.5 us (18%)
  blocking collectives  50.7 us (10%)
  other arithmetic  45.2 us (9%)
  starting transfers between devices  30.8 us (6%)
  matrix products  19.7 us (4%)
  between operations  15 us (3%)
    all_to_all x1, waiting for transfers between devices, body(): lax.all_to_all(send_rows, 'group', split_axis=0, concat_axis=0, tiled=True)  91.8 us
    another operation x2, Pallas kernels  79.2 us
    psum x1, waiting for transfers between devices, body(): moment, col_mass = lax.psum((moment, mass_local), 'rep')  36.8 us
    psum x3, blocking collectives, body(): lax.psum(jnp.sum(balanced_transport_routine * sample_wise, axis=1), 'proto')  30.6 us
    gather x1, local copies, waits for them, and re-layouts, body(): sorted_slot = jnp.take(sort_key, order)  23 us
    gather x1, local copies, waits for them, and re-layouts, body(): sorted_rows = jnp.take(arrived, order, axis=0)  22.7 us
    all_to_all x1, starting transfers between devices, body(): lax.all_to_all((FPC * plan_slots).reshape(groups, capacity, fine_local),...  18.8 us
    unnamed x5, other arithmetic  14.4 us
  transfers between devices with their start and end apart: 4, of which 3 were waited for; matrix products, arithmetic and copies ran while one was open for 18% of the time, Pallas kernels for 1%

commit v1 on v0

v1 whole, which is shorter than its diff:
```python
import functools

import jax
import jax.numpy as jnp
from jax import lax
from jax.experimental import pallas as pl
from jax.experimental.pallas import tpu as pltpu
from jax.sharding import PartitionSpec as P

FPC = 64
ITERS = 3
SHARPNESS = 0.03
EXTRA = 16
F32, BF16 = jnp.float32, jnp.bfloat16
MESH = pl.DeviceIdType.MESH
VM = pl.BlockSpec(memory_space=pltpu.VMEM)
NT = (((1,), (1,)), ((), ()))


def unit(values):
    return values * lax.rsqrt(jnp.mean(values * values, axis=-1, keepdims=True) + 1e-06)


def remote(src, dst, send_sem, recv_sem, where):
    return pltpu.make_async_remote_copy(
        src_ref=src, dst_ref=dst, send_sem=send_sem, recv_sem=recv_sem,
        device_id=where, device_id_type=MESH)


def greet(peers):
    barrier = pltpu.get_barrier_semaphore()
    for peer in peers:
        pl.semaphore_signal(barrier, inc=1, device_id=peer, device_id_type=MESH)
    pl.semaphore_wait(barrier, len(peers))


def others(name):
    n, me = lax.axis_size(name), lax.axis_index(name)
    return [{name: lax.rem(me + k, n)} for k in range(1, n)]


def dispatch_kernel(groups, protos, cap, tile, width, dest_ref, slot_ref, xa_ref, xb_ref, w_ref,
                    got_ref, gotw_ref, send, ssem, rsem, wssem, wrsem, lsem):
    me, mp = lax.axis_index("group"), lax.axis_index("proto")
    half = cap // 2
    wide = xa_ref.shape[1]
    off = width - wide
    greet(others("group") + others("proto"))
    wcopies = []
    for k in range(1, protos):
        to = lax.rem(mp + k, protos)
        c = remote(w_ref.at[to], gotw_ref.at[mp], wssem.at[k], wrsem.at[k], {"proto": to})
        c.start()
        wcopies.append(c)
    own = pltpu.make_async_copy(w_ref.at[mp], gotw_ref.at[mp], lsem)
    own.start()
    copies = []
    rows = dest_ref.shape[1]
    row16 = lax.broadcasted_iota(jnp.int32, (EXTRA, tile), 0)
    order = [groups // 2] + [k for k in range(1, groups) if k != groups // 2] + [0]
    for k in order:
        to = lax.rem(me + k, groups)

        buf = got_ref.at[me] if k == 0 else send.at[k]
        codes = jnp.zeros((EXTRA, tile), F32)
        for t in range(half // tile):
            at = lax.broadcasted_iota(jnp.int32, (tile, rows), 0) + (to * cap + t * tile)
            oa = jnp.where(at == dest_ref[...], 1.0, 0.0).astype(BF16)
            ob = jnp.where(at + half == dest_ref[...], 1.0, 0.0).astype(BF16)
            a = jnp.dot(oa, xa_ref[...], preferred_element_type=F32)
            b = jnp.dot(ob, xb_ref[...], preferred_element_type=F32)
            sa = lax.dot_general(slot_ref[...], oa, NT, preferred_element_type=F32)
            sb = lax.dot_general(slot_ref[...], ob, NT, preferred_element_type=F32)
            codes = jnp.where(row16 == t, sa, codes)
            codes = jnp.where(row16 == half // tile + t, sb, codes)
            r = pl.ds(t * tile, tile)
            buf[r, :off] = a[:, :off].astype(BF16)
            buf[r, off:wide] = (a[:, off:] + b[:, :wide - off]).astype(BF16)
            buf[r, wide:] = b[:, wide - off:].astype(BF16)
        buf[pl.ds(half, EXTRA), :tile] = codes.astype(BF16)
        buf[pl.ds(half, EXTRA), tile:] = jnp.zeros((EXTRA, width - tile), BF16)
        if k:
            c = remote(send.at[k], got_ref.at[me], ssem.at[k], rsem.at[k], {"group": to})
            c.start()
            copies.append(c)
    own.wait()
    for c in wcopies + copies:
        c.wait()


def sinkhorn_kernel(groups, protos, reps, cap, tile, scale, got_ref, w_ref,
                    plan_ref, mass_ref, slot_ref, r_ref,
                    part, prec, member, xs, xr, kall,
                    psem, prsem, ksem, krsem, xsem, xrsem):
    mp, mr = lax.axis_index("proto"), lax.axis_index("rep")
    half = cap // 2
    total = groups * cap
    width = got_ref.shape[2]
    wide = r_ref.shape[1]
    off = width - wide
    cols = w_ref.shape[1]
    fine = FPC // protos
    clusters = cols // fine
    greet(others("proto") + others("rep"))
    for g in range(groups):
        a = got_ref[g, :half, :wide]
        b = got_ref[g, :half, off:].astype(F32)
        r_ref[pl.ds(g * cap, half), :] = a
        r_ref[pl.ds(g * cap + half, half), :] = pltpu.roll(b, wide - (width // 2 - off), 1).astype(BF16)
        for u in range(cap // tile):
            s = got_ref[g, pl.ds(half, EXTRA), :tile].astype(F32)[u:u + 1, :]
            slot_ref[:, pl.ds(g * cap + u * tile, tile)] = jnp.broadcast_to(s, (8, tile)).astype(jnp.int32)

    chunk = 512
    step = 256
    per = step // fine

    def score(to, c):
        lanes = pl.ds(pl.multiple_of(c * chunk, chunk), chunk)
        rows = r_ref[lanes, :]
        slots = jnp.broadcast_to(slot_ref[:1, lanes], (fine, chunk))
        acc = jnp.zeros((fine, chunk), F32)
        for j in range(cols // step):
            s = lax.dot_general(w_ref[to, pl.ds(j * step, step), :], rows, NT, preferred_element_type=F32)
            for i in range(per):
                acc = jnp.where(slots == j * per + i + 1, s[i * fine:(i + 1) * fine], acc)
        return lanes, acc

    copies = []
    for k in list(range(1, protos)) + [0]:
        to = lax.rem(mp + k, protos)

        @pl.loop(0, total // chunk)
        def _(c):
            lanes, acc = score(to, c)
            part[k, :, lanes] = acc

        if k:
            c = remote(part.at[k], prec.at[k], psem.at[k], prsem.at[k], {"proto": to})
            c.start()
            copies.append(c)
    for c in copies:
        c.wait()
    live = slot_ref[:1, :] > 0
    s = part[0]
    for k in range(1, protos):
        s = s + prec[k]
    kern = jnp.where(live, jnp.exp(s * scale), 0.0).astype(BF16)
    kall[mp] = kern
    copies = []
    for k in range(1, protos):
        to = lax.rem(mp + k, protos)
        c = remote(kall.at[mp], kall.at[mp], ksem.at[k], krsem.at[k], {"proto": to})
        c.start()
        copies.append(c)
    width_m = member.shape[0]
    cl = lax.broadcasted_iota(jnp.int32, (width_m, chunk), 0) + 1

    @pl.loop(0, total // chunk)
    def _(c):
        lanes = pl.ds(pl.multiple_of(c * chunk, chunk), chunk)
        member[:, lanes] = jnp.where(slot_ref[:1, lanes] == cl, 1.0, 0.0).astype(BF16)

    for c in copies:
        c.wait()

    def exchange(n, value):
        xs[n] = value
        cs = []
        for k in range(1, reps):
            to = lax.rem(mr + k, reps)
            c = remote(xs.at[n], xr.at[n, k], xsem.at[n, k], xrsem.at[n, k], {"rep": to})
            c.start()
            cs.append(c)
        for k in range(1, reps):
            cs[k - 1].wait()
            value = value + xr[n, k]
        return value

    def pad8(v):
        return jnp.concatenate([v, jnp.zeros((8, width_m), F32)], axis=0)

    nch = total // chunk
    livef = live.astype(F32)

    def piece(c):
        return slice(c * chunk, (c + 1) * chunk)

    def kern_of(c):
        return kall[:, :, piece(c)].reshape(FPC, chunk).astype(F32)

    weights = [livef[:, piece(c)] for c in range(nch)]
    counts = lax.dot_general(jnp.broadcast_to(livef, (16, total)).astype(BF16), member[...], NT,
                             preferred_element_type=F32)[:8]
    for n in range(ITERS):
        col = jnp.zeros((FPC, width_m), F32)
        for c in range(nch):
            kw = (kern_of(c) * weights[c]).astype(BF16)
            col = col + lax.dot_general(kw, member[:, piece(c)], NT, preferred_element_type=F32)
        if n == 0:
            both = exchange(0, jnp.concatenate([col, counts], axis=0))
            col, count = both[:FPC], both[FPC:FPC + 1]
        else:
            col = exchange(n, pad8(col))[:FPC]
        occ = jnp.broadcast_to(count, col.shape) > 0
        scal = jnp.where(occ, count / FPC / jnp.where(occ, col, 1.0), 0.0)
        hi = scal.astype(BF16)
        lo = (scal - hi.astype(F32)).astype(BF16)
        mass = jnp.zeros((FPC, width_m), F32)
        for c in range(nch):
            m = member[:, piece(c)]
            sw = jnp.dot(hi, m, preferred_element_type=F32) + jnp.dot(lo, m, preferred_element_type=F32)
            ks = kern_of(c) * sw
            row = jnp.sum(ks, axis=0, keepdims=True)
            lv = livef[:, piece(c)] > 0
            weights[c] = jnp.where(lv, 1.0 / jnp.where(lv, row, 1.0), 0.0)
            if n == ITERS - 1:
                low = (ks * weights[c]).astype(BF16)
                plan_ref[:, piece(c)] = low
                mass = mass + lax.dot_general(low, m, NT, preferred_element_type=F32)
    mass_ref[...] = exchange(ITERS, pad8(mass))[:FPC]


def update_kernel(groups, protos, reps, cap, fw, plan_ref, slot_ref, r_ref, mass_ref, proto_ref, dest_ref,
                  new_ref, codes_ref, send, mrec, crec, ss, ssr,
                  csem, crsem, msem, mrsem, lsem, ssem, ssrsem):
    mg, mp, mr = lax.axis_index("group"), lax.axis_index("proto"), lax.axis_index("rep")
    total = groups * cap
    fine = FPC // protos
    packed = send.shape[1]
    width = send.shape[2]
    wide = r_ref.shape[1]
    off = width - wide
    shift = width // 2 - off
    share = protos // reps
    half_to = lax.rem(mp, reps)
    j_mine = mp // reps
    peers = others("group")
    for a in range(reps):
        for b in range(protos):
            if a or b:
                peers.append({"rep": lax.rem(mr + a, reps), "proto": lax.rem(mp + b, protos)})
    greet(peers)
    copies = []
    f_rows = pl.ds(pl.multiple_of(mp * fine, fine), fine)
    for k in range(1, groups):
        to = lax.rem(mg + k, groups)
        c = remote(plan_ref.at[f_rows, pl.ds(pl.multiple_of(to * cap, cap), cap)], crec.at[mg],
                   csem.at[k], crsem.at[k], {"group": to})
        c.start()
        copies.append(c)
    crec_own = plan_ref[f_rows, pl.ds(pl.multiple_of(mg * cap, cap), cap)]
    crec[mg] = crec_own

    block = 256
    per = block // fine
    chunk = 1024
    lane = lax.broadcasted_iota(jnp.int32, (block, off), 1)

    def moment(to, first):
        plan_rows = pl.ds(pl.multiple_of(to * fine, fine), fine)
        acc = jnp.zeros((block, wide), F32)
        for c in range(total // chunk):
            lanes = slice(c * chunk, (c + 1) * chunk)
            plan = plan_ref[plan_rows, lanes].astype(F32)
            slots = jnp.broadcast_to(slot_ref[:1, lanes], (fine, chunk)) - first
            a = jnp.concatenate(
                [jnp.where(slots == i + 1, plan, 0.0).astype(BF16) for i in range(per)], axis=0)
            acc = acc + jnp.dot(a, r_ref[lanes, :], preferred_element_type=F32)
        return acc

    slot_out = mr * share + j_mine
    is_self = half_to == mr
    mcopies = []
    for k in list(range(1, protos)) + [0]:
        to = lax.rem(mp + k, protos)

        @pl.loop(0, packed // block)
        def _(t):
            a = moment(to, t * per)
            b = pltpu.roll(moment(to, t * per + packed // fine), shift, 1)
            r = pl.ds(pl.multiple_of(t * block, block), block)
            send[k, r, :off] = a[:, :off].astype(BF16)
            send[k, r, off:wide] = jnp.where(lane < shift, a[:, off:], b[:, :wide - off]).astype(BF16)
            send[k, r, wide:] = b[:, wide - off:].astype(BF16)

        c = remote(send.at[k], mrec.at[slot_out], msem.at[k], mrsem.at[slot_out],
                   {"rep": half_to, "proto": to})
        if k:
            c.start()
            mcopies.append(c)
        else:
            @pl.when(is_self)
            def _():
                l = pltpu.make_async_copy(send.at[0], mrec.at[slot_out], lsem)
                l.start()
                l.wait()

            @pl.when(jnp.logical_not(is_self))
            def _():
                c.start()
                c.wait_send()

    for c in copies:
        c.wait()
    nrow = dest_ref.shape[0]
    rt = 256

    @pl.loop(0, nrow // rt)
    def _(t):
        r = pl.ds(pl.multiple_of(t * rt, rt), rt)
        acc = jnp.zeros((rt, fine), F32)
        d = jnp.broadcast_to(dest_ref[r, :], (rt, cap))
        for g in range(groups):
            hot = jnp.where(d == lax.broadcasted_iota(jnp.int32, (rt, cap), 1) + g * cap, 1.0, 0.0)
            acc = acc + lax.dot_general(hot.astype(BF16), crec[g], NT, preferred_element_type=F32)
        codes_ref[r, :] = acc * FPC

    for c in mcopies:
        c.wait_send()
    for a in range(reps):
        for j in range(share):
            s = a * share + j
            mine = jnp.logical_and(a == mr, j * reps + mr == mp)

            @pl.when(jnp.logical_not(mine))
            def _():
                remote(send.at[0], mrec.at[s], msem.at[0], mrsem.at[s],
                       {"rep": lax.rem(mr + 1, reps)}).wait_recv()

    lane2 = lax.broadcasted_iota(jnp.int32, (128, off), 1)
    eye = lax.broadcasted_iota(jnp.int32, (128, 128), 0) == lax.broadcasted_iota(jnp.int32, (128, 128), 1)
    n128 = packed // 128
    sums = []
    for t in range(n128):
        r = slice(t * 128, (t + 1) * 128)
        v = []
        for j in range(share):
            x = mrec[j, r, :].astype(F32)
            for a in range(1, reps):
                x = x + mrec[a * share + j, r, :].astype(F32)
            v.append(x)
        t0, t1 = v
        b = pltpu.roll(t1[:, :wide], shift, 1)
        u = pltpu.roll(t0[:, off:], wide - shift, 1)
        first = [t0[:, :off], jnp.where(lane2 < shift, t0[:, off:wide], b[:, :wide - off]), b[:, wide - off:]]
        second = [u[:, :off], jnp.where(lane2 < shift, u[:, off:wide], t1[:, off:wide]), t1[:, wide:]]
        for h, vals in enumerate((first, second)):
            rr = slice(h * packed + t * 128, h * packed + (t + 1) * 128)
            mom = jnp.concatenate(vals, axis=1)
            up = (proto_ref[rr, :].astype(F32) + mom) / (1.0 + mass_ref[rr, :])
            new_ref[rr, :] = up
            q = jnp.sum(up * up, axis=1, keepdims=True)
            sums.append((h * n128 + t, jnp.sum(jnp.where(eye, jnp.broadcast_to(q, (128, 128)), 0.0), axis=0, keepdims=True)))
    sums.sort(key=lambda e: e[0])
    own = jnp.concatenate([e[1] for e in sums], axis=0)
    ss[...] = own
    cs = []
    for k in range(1, reps):
        c = remote(ss, ssr.at[k], ssem.at[k], ssrsem.at[k], {"rep": lax.rem(mr + k, reps)})
        c.start()
        cs.append(c)
    for k in range(1, reps):
        cs[k - 1].wait()
        own = own + ssr[k]
    inv = lax.rsqrt(own / (fw * protos) + 1e-06)
    for t in range(2 * n128):
        rr = slice(t * 128, (t + 1) * 128)
        f = jnp.sum(jnp.where(eye, jnp.broadcast_to(inv[t:t + 1, :], (128, 128)), 0.0), axis=1, keepdims=True)
        new_ref[rr, :] = new_ref[rr, :] * f


def body(embeddings, labels, cluster_place, row_counts, prototypes):
    rows, dim = embeddings.shape
    groups, protos, reps = lax.axis_size("group"), lax.axis_size("proto"), lax.axis_size("rep")
    mp, mr = lax.axis_index("proto"), lax.axis_index("rep")
    cap = rows // max(groups // 4, 2)
    clusters, fine, _ = prototypes.shape
    share = protos // reps
    fw = dim // protos
    wide = -(-fw // 128) * 128
    width = 2 * fw
    off = width - wide
    half = cap // 2
    tile = min(256, half)
    total = groups * cap
    cols = clusters * fine

    def quarter(p):
        return (p % reps) * share + p // reps

    place = jnp.sum(jnp.where(labels[:, None] == jnp.arange(cluster_place.shape[0])[None, :],
                              cluster_place[None, :], 0), axis=1)
    target, slot = place // clusters, place % clusters
    live = jnp.arange(rows) < row_counts[0]
    choose = (target[:, None] == jnp.arange(groups)[None, :]) & live[:, None]
    running = jnp.cumsum(choose.astype(jnp.int32), axis=0) - 1
    position = jnp.sum(jnp.where(choose, running, 0), axis=1)
    dest = jnp.where(live, target * cap + position, -1).astype(jnp.int32)
    slot16 = jnp.broadcast_to((slot + 1).astype(BF16)[None, :], (16, rows))
    rows_f = embeddings.astype(F32)
    inv = lax.rsqrt(jnp.mean(rows_f * rows_f, axis=-1, keepdims=True) + 1e-06)
    q = lax.rem(mp, reps) * share + mp // reps
    mine = lax.dynamic_slice_in_dim(embeddings, q * fw, fw, 1).astype(F32)
    xq = (mine * inv).astype(BF16)
    xa = jnp.pad(xq, ((0, 0), (0, wide - fw)))
    xb = jnp.pad(xq, ((0, 0), (wide - fw, 0)))
    unit_p = unit(prototypes.astype(F32)).astype(BF16).reshape(cols, dim)
    w = jnp.stack([jnp.pad(unit_p[:, quarter(p) * fw:(quarter(p) + 1) * fw], ((0, 0), (0, wide - fw)))
                   for p in range(protos)])
    dma, sds = pltpu.SemaphoreType.DMA, jax.ShapeDtypeStruct
    params = functools.partial(pltpu.CompilerParams, has_side_effects=True, vmem_limit_bytes=60 * 2**20)
    got, gotw = pl.pallas_call(
        functools.partial(dispatch_kernel, groups, protos, cap, tile, width),
        out_shape=(sds((groups, half + EXTRA, width), BF16), sds((protos, cols, wide), BF16)),
        in_specs=[VM] * 5,
        out_specs=(VM, VM),
        scratch_shapes=[pltpu.VMEM((groups, half + EXTRA, width), BF16),
                        dma((groups,)), dma((groups,)), dma((protos,)), dma((protos,)), dma],
        compiler_params=params(collective_id=0),
    )(dest[None, :], slot16, xa, xb, w)
    plan, mass, slots, r = pl.pallas_call(
        functools.partial(sinkhorn_kernel, groups, protos, reps, cap, tile, 1.0 / (dim * SHARPNESS)),
        out_shape=(sds((FPC, total), BF16), sds((FPC, 128), F32), sds((8, total), jnp.int32),
                   sds((total, wide), BF16)),
        in_specs=[VM] * 2,
        out_specs=(VM,) * 4,
        scratch_shapes=[pltpu.VMEM((protos, fine, total), F32), pltpu.VMEM((protos, fine, total), F32),
                        pltpu.VMEM((128, total), BF16),
                        pltpu.VMEM((ITERS + 1, FPC + 8, 128), F32),
                        pltpu.VMEM((ITERS + 1, reps, FPC + 8, 128), F32),
                        pltpu.VMEM((protos, fine, total), BF16),
                        dma((protos,)), dma((protos,)), dma((protos,)), dma((protos,)),
                        dma((ITERS + 1, reps)), dma((ITERS + 1, reps))],
        compiler_params=params(collective_id=1),
    )(got, gotw)
    mass_col = lax.dynamic_slice_in_dim(mass, mp * fine, fine, 0)[:, :clusters].T.reshape(cols, 1)
    hw = dim // reps
    proto_half = lax.dynamic_slice_in_dim(prototypes, mr * hw, hw, 2).reshape(cols, hw)
    new, codes = pl.pallas_call(
        functools.partial(update_kernel, groups, protos, reps, cap, fw),
        out_shape=(sds((cols, hw), F32), sds((rows, fine), F32)),
        in_specs=[VM] * 6,
        out_specs=(VM, VM),
        scratch_shapes=[pltpu.VMEM((protos, cols // 2, width), BF16),
                        pltpu.VMEM((reps * share, cols // 2, width), BF16),
                        pltpu.VMEM((groups, fine, cap), BF16),
                        pltpu.VMEM((cols // 128, 128), F32), pltpu.VMEM((reps, cols // 128, 128), F32),
                        dma((groups,)), dma((groups,)), dma((protos,)), dma((reps * share,)), dma,
                        dma((reps,)), dma((reps,))],
        compiler_params=params(collective_id=2),
    )(plan, slots, r, mass_col, proto_half, dest[:, None])
    return new.reshape(clusters, fine, hw), codes


def solution(mesh):
    return jax.shard_map(
        body,
        mesh=mesh,
        in_specs=(
            P(("rep", "group"), None),
            P(("rep", "group")),
            P(),
            P(("rep", "group")),
            P("group", "proto", None),
        ),
        out_specs=(P("group", "proto", "rep"), P(("rep", "group"), "proto")),
        check_vma=False,
    )
```

time: 490 us -> 157 us (0.32)
  waiting for transfers between devices: 131 us -> 0 us
  local copies, waits for them, and re-layouts: 109 us -> 12.8 us
  blocking collectives: 50.7 us -> 0 us
  Pallas kernels: 86.5 us -> 129 us
  other arithmetic: 45.2 us -> 13 us
  starting transfers between devices: 30.8 us -> 0 us
  matrix products: 19.7 us -> 0 us
  between operations: 15 us -> 1.47 us
    pallas_call x0 -> x3, Pallas kernels: none -> 129 us  [the longest x1 45.7 us: body(): pl.pallas_call(functools.partial(sinkhorn_kernel, groups, protos, reps, c...]
    all_to_all x3 -> x0, waiting for transfers between devices: 94 us -> none  [the longest x1 91.8 us: body(): lax.all_to_all(send_rows, 'group', split_axis=0, concat_axis=0, tiled=True)]
    another operation x2 -> x0, Pallas kernels: 79.2 us -> none
    gather x4 -> x0, local copies, waits for them, and re-layouts: 71.9 us -> none  [the longest x1 23 us: body(): sorted_slot = jnp.take(sort_key, order)]
    psum x7 -> x0, blocking collectives: 50.7 us -> none  [the longest x3 30.6 us: body(): lax.psum(jnp.sum(balanced_transport_routine * sample_wise, axis=1), 'proto')]
    psum x1 -> x0, waiting for transfers between devices: 36.8 us -> none  [body(): moment, col_mass = lax.psum((moment, mass_local), 'rep')]
    all_to_all x3 -> x0, starting transfers between devices: 30.5 us -> none  [the longest x1 18.8 us: body(): lax.all_to_all((FPC * plan_slots).reshape(groups, capacity, fine_local),...]
    dot_general x7 -> x0, matrix products: 19.7 us -> none  [the longest x3 10.6 us: column_part(): lax.dot_general(member_f, balanced_transport_routine * sample_importance[...]
  transfers between devices with their start and end apart: 4 -> 0, of which waited for: 3 -> 0; matrix products, arithmetic and copies ran while one was open for 18% -> 0% of each run, Pallas kernels for 1% -> 0%
where the time goes in v1:
time: 157 us; the launch traced here: 156 us
  Pallas kernels  129 us (82%)
  other arithmetic  13 us (8%)
  local copies, waits for them, and re-layouts  12.8 us (8%)
    pallas_call x1, Pallas kernels, body(): pl.pallas_call(functools.partial(sinkhorn_kernel, groups, protos, reps, c...  45.7 us
    pallas_call x1, Pallas kernels, body(): pl.pallas_call(functools.partial(dispatch_kernel, groups, protos, cap, ti...  42.1 us
    pallas_call x1, Pallas kernels, body(): pl.pallas_call(functools.partial(update_kernel, groups, protos, reps, cap...  41.3 us
    unnamed x10, local copies, waits for them, and re-layouts  4.86 us
    select_n x2, other arithmetic, body(): dest = jnp.where(live, target * cap + position, -1).astype(jnp.int32)  3.58 us

profile of v1, /device:TPU:0, one launch (start us, length us, event | category | flops | bytes accessed | tf_op | source)
XLA Modules:
  0.0 156.4 jit_solution(7106767355853119386)
XLA Ops:
  0.6 2.6 %multiply_reduce_fusion = f32[2048]{0:T(1024)S(1)} fusion(bf16[2048,768]{1,0:T(8,128)(2,1)} %param.5), kind=kLoop, calls=%fused_computation | loop fusion | flops 4716544 | bytes 3153920 | tf_op jit(solution)/shard_map/reduce_sum | solution.py:402
  3.2 2.1 %multiply_convert_fusion = bf16[2048,192]{1,0:T(8,128)(2,1)S(1)} fusion(f32[2048]{0:T(1024)S(1)} %add_rsqrt_fusion.1, bf16[2048,768]{1,0:T(8,128)(2,1)} %param.5, s32[]{:T(128)S(6)} %select_n.89), kind=kLoop, calls=%fused_computation.6 | loop fusion | flops 1179648 | bytes 1581060 | tf_op jit(solution)/shard_map/convert_element_type | solution.py:405
  5.3 0.0 copy-start.1
  5.3 0.0 copy-start.2
  5.3 0.0 copy-start
  5.4 1.8 %fusion.21 = (bf16[2048,256]{1,0:T(8,128)(2,1)}, bf16[2048,256]{1,0:T(8,128)(2,1)}) fusion(bf16[2048,192]{1,0:T(8,128)(2,1)S(1)} %multiply_convert_fusion), kind=kLoop, calls=%fused_computation.66 | loop fusion | bytes 2883584 | tf_op jit(solution)/shard_map/jit(_pad)/pad | solution.py:407
  7.2 0.7 select_reduce_fusion
  8.6 1.2 reduce-window.6
  9.8 0.2 slice_reduce_fusion
  10.0 0.2 reduce-window.9
  10.2 0.1 add_bitcast_fusion
  10.4 0.6 compare_select_fusion.dest_ref
  11.0 0.4 fusion
  11.4 0.3 fusion.1
  11.7 0.0 copy-start.3
  11.7 0.5 fusion.20
  12.2 0.2 pad_bitcast_fusion
  12.4 0.2 fusion.7
  12.6 1.6 %pad_maximum_fusion.w_ref = bf16[4,1024,256]{2,1,0:T(8,128)(2,1)} fusion(bf16[1,1024,256]{2,1,0:T(8,128)(2,1)S(1)} %get-tuple-element.31, bf16[1,1024,256]{2,1,0:T(8,128)(2,1)S(1)} %get-tuple-element.32, bf16[1,1024,256]{2,1,0:T(8,128)(2,1)S(1)} %get-tuple-element.34, bf16[1,1024,256]{2,1,0:T(8,128)(2,1)S(1)} %get-tuple-element.33), kind=kLoop, calls=%fused_computation.5 | loop fusion | flops 3145728 | bytes 4194304 | tf_op jit(solution)/shard_map/stack | solution.py:409
  14.2 0.6 broadcast_in_dim.23.slot_ref
  14.8 42.1 %shard_map.68 = (bf16[4,528,384]{2,1,0:T(8,128)(2,1)}, bf16[4,1024,256]{2,1,0:T(8,128)(2,1)}) custom-call(s32[1,2048]{1,0:T(1,128)} %compare_select_fusion.dest_ref, bf16[16,2048]{1,0:T(8,128)(2,1)} %broadcast_in_dim.23.slot_ref, bf16[2048,256]{1,0:T(8,128)(2,1)} %get-tuple-element.28.xa_ref, bf16[2048,256]{1,0:T(8,128)(2,1)} %get-tuple-element.27.xb_ref, ...), custom_call_target="tpu_custom_call" | custom-call | tf_op jit(solution)/shard_map/pallas_call | solution.py:413
  57.0 45.7 %shard_map.69 = (bf16[64,4096]{1,0:T(8,128)(2,1)}, f32[64,128]{1,0:T(8,128)}, s32[8,4096]{1,0:T(8,128)}, bf16[4096,256]{1,0:T(8,128)(2,1)}) custom-call(bf16[4,528,384]{2,1,0:T(8,128)(2,1)} %get-tuple-element.10.got_ref, bf16[4,1024,256]{2,1,0:T(8,128)(2,1)} %get-tuple-element.11.w_ref), custom_call_target="tpu_custom_call" | custom-call | tf_op jit(solution)/shard_map/pallas_call | solution.py:422
  102.7 0.7 dynamic-slice_bitcast_fusion
  103.4 0.1 copy.17
  103.5 1.1 reshape.221.mass_ref
  104.6 0.4 copy.22
  105.0 1.4 copy.18
  106.3 2.9 %fusion.5.dest_ref = s32[2048,1]{1,0:T(8,128)} fusion(s32[2048,1]{1,0:T(8,128)S(1)} %copy.22, s32[2048,1]{1,0:T(8,128)} %copy.18, s32[]{:T(128)} %bitcast.52), kind=kLoop, calls=%fused_computation.16 | loop fusion | flops 38912 | bytes 24580 | tf_op jit(solution)/shard_map/jit(_where)/select_n | solution.py:399
  109.3 1.0 constant_dynamic-slice_fusion
  110.2 41.3 %shard_map.70 = (f32[1024,384]{1,0:T(8,128)}, f32[2048,16]{1,0:T(8,128)}) custom-call(bf16[64,4096]{1,0:T(8,128)(2,1)} %get-tuple-element.12.plan_ref, s32[8,4096]{1,0:T(8,128)} %get-tuple-element.13.slot_ref, bf16[4096,256]{1,0:T(8,128)(2,1)} %get-tuple-element.14.r_ref, f32[1024,1]{1,0:T(8,128)} %reshape.221.mass_ref, bf16[1024,384]{1,0:T(8,128)(2,1)} %bitcast.55, ...), custom_call_target="tpu_custom_call" | custom-call | tf_op jit(solution)/shard_map/pallas_call | solution.py:440
  151.6 2.2 %copy.24 = f32[2048,16]{0,1:T(8,128)} copy(f32[2048,16]{1,0:T(8,128)} %get-tuple-element.23) | data formatting | bytes 262144
  153.8 2.7 %copy.29 = f32[64,16,384]{2,1,0:T(8,128)} copy(f32[64,16,384]{2,1,0:T(8,128)} %bitcast.56) | data formatting | bytes 3145728
  (12 shorter events, 0.1 us)
Async XLA Ops:
  5.3 1.9 %copy-start.1 = (s32[2048]{0:T(1024)S(1)}, s32[2048]{0:T(1024)}, u32[]{:S(2)}) copy-start(s32[2048]{0:T(1024)} %param.6) | copy-start | bytes 24580
  5.3 1.9 %copy-start.2 = (s32[256]{0:T(256)S(1)}, s32[256]{0:T(256)}, u32[]{:S(2)}) copy-start(s32[256]{0:T(256)} %param.7) | copy-start | bytes 3076
  5.3 5.7 %copy-start = (bf16[64,16,768]{2,1,0:T(8,128)(2,1)S(1)}, bf16[64,16,768]{2,1,0:T(8,128)(2,1)}, u32[]{:S(2)}) copy-start(bf16[64,16,768]{2,1,0:T(8,128)(2,1)} %param.9) | copy-start | bytes 4718596
  11.7 0.7 copy-start.3

commit v2 on v1

--- a/solution.py
+++ b/solution.py
@@ -39,29 +39,27 @@
     return [{name: lax.rem(me + k, n)} for k in range(1, n)]
 
 
-def dispatch_kernel(groups, protos, cap, tile, width, dest_ref, slot_ref, xa_ref, xb_ref, w_ref,
-                    got_ref, gotw_ref, send, ssem, rsem, wssem, wrsem, lsem):
-    me, mp = lax.axis_index("group"), lax.axis_index("proto")
+def sinkhorn_kernel(groups, protos, reps, cap, tile, width, fw, scale,
+                    dest_ref, slot_in_ref, xa_ref, xb_ref, proto_ref,
+                    plan_ref, mass_ref, slot_ref, r_ref,
+                    got, send, wsend, wgot, w_ref, part, prec, member, xs, xr, kall,
+                    ssem, rsem, wssem, wrsem, psem, prsem, ksem, krsem, xsem, xrsem):
+    me, mp, mr = lax.axis_index("group"), lax.axis_index("proto"), lax.axis_index("rep")
     half = cap // 2
-    wide = xa_ref.shape[1]
+    total = groups * cap
+    wide = r_ref.shape[1]
     off = width - wide
-    greet(others("group") + others("proto"))
-    wcopies = []
-    for k in range(1, protos):
-        to = lax.rem(mp + k, protos)
-        c = remote(w_ref.at[to], gotw_ref.at[mp], wssem.at[k], wrsem.at[k], {"proto": to})
-        c.start()
-        wcopies.append(c)
-    own = pltpu.make_async_copy(w_ref.at[mp], gotw_ref.at[mp], lsem)
-    own.start()
-    copies = []
+    shift = fw - off
+    cols, dim = proto_ref.shape
+    fine = FPC // protos
+    share = protos // reps
     rows = dest_ref.shape[1]
     row16 = lax.broadcasted_iota(jnp.int32, (EXTRA, tile), 0)
-    order = [groups // 2] + [k for k in range(1, groups) if k != groups // 2] + [0]
-    for k in order:
+    greet(others("group") + others("proto") + others("rep"))
+
+    def bucket(k):
         to = lax.rem(me + k, groups)
-
-        buf = got_ref.at[me] if k == 0 else send.at[k]
+        buf = got.at[me] if k == 0 else send.at[k]
         codes = jnp.zeros((EXTRA, tile), F32)
         for t in range(half // tile):
             at = lax.broadcasted_iota(jnp.int32, (tile, rows), 0) + (to * cap + t * tile)
@@ -69,8 +67,8 @@
             ob = jnp.where(at + half == dest_ref[...], 1.0, 0.0).astype(BF16)
             a = jnp.dot(oa, xa_ref[...], preferred_element_type=F32)
             b = jnp.dot(ob, xb_ref[...], preferred_element_type=F32)
-            sa = lax.dot_general(slot_ref[...], oa, NT, preferred_element_type=F32)
-            sb = lax.dot_general(slot_ref[...], ob, NT, preferred_element_type=F32)
+            sa = lax.dot_general(slot_in_ref[...], oa, NT, preferred_element_type=F32)
+            sb = lax.dot_general(slot_in_ref[...], ob, NT, preferred_element_type=F32)
             codes = jnp.where(row16 == t, sa, codes)
             codes = jnp.where(row16 == half // tile + t, sb, codes)
             r = pl.ds(t * tile, tile)
@@ -80,89 +78,126 @@
         buf[pl.ds(half, EXTRA), :tile] = codes.astype(BF16)
         buf[pl.ds(half, EXTRA), tile:] = jnp.zeros((EXTRA, width - tile), BF16)
         if k:
-            c = remote(send.at[k], got_ref.at[me], ssem.at[k], rsem.at[k], {"group": to})
+            c = remote(send.at[k], got.at[me], ssem.at[k], rsem.at[k], {"group": to})
             c.start()
-            copies.append(c)
-    own.wait()
-    for c in wcopies + copies:
-        c.wait()
-
-
-def sinkhorn_kernel(groups, protos, reps, cap, tile, scale, got_ref, w_ref,
-                    plan_ref, mass_ref, slot_ref, r_ref,
-                    part, prec, member, xs, xr, kall,
-                    psem, prsem, ksem, krsem, xsem, xrsem):
-    mp, mr = lax.axis_index("proto"), lax.axis_index("rep")
-    half = cap // 2
-    total = groups * cap
-    width = got_ref.shape[2]
-    wide = r_ref.shape[1]
-    off = width - wide
-    cols = w_ref.shape[1]
-    fine = FPC // protos
-    clusters = cols // fine
-    greet(others("proto") + others("rep"))
-    for g in range(groups):
-        a = got_ref[g, :half, :wide]
-        b = got_ref[g, :half, off:].astype(F32)
-        r_ref[pl.ds(g * cap, half), :] = a
-        r_ref[pl.ds(g * cap + half, half), :] = pltpu.roll(b, wide - (width // 2 - off), 1).astype(BF16)
-        for u in range(cap // tile):
-            s = got_ref[g, pl.ds(half, EXTRA), :tile].astype(F32)[u:u + 1, :]
-            slot_ref[:, pl.ds(g * cap + u * tile, tile)] = jnp.broadcast_to(s, (8, tile)).astype(jnp.int32)
+            return c
+
+    def spread_protos():
+        wt = 128
+        lane = lax.broadcasted_iota(jnp.int32, (wt, off), 1)
+
+        @pl.loop(0, cols // 2 // wt)
+        def _(t):
+            ra = pl.ds(pl.multiple_of(t * wt, wt), wt)
+            rb = pl.ds(pl.multiple_of(t * wt + cols // 2, wt), wt)
+            ua, ub = unit(proto_ref[ra, :].astype(F32)), unit(proto_ref[rb, :].astype(F32))
+            for q in range(protos):
+                p = (q % share) * reps + q // share
+                base = q * fw // 128 * 128
+                o = q * fw - base
+                a, b = ua[:, base:base + wide], ub[:, base:base + wide]
+                a = a if o == 0 else pltpu.roll(a, wide - o, 1)
+                b = b if o == shift else pltpu.roll(b, (shift - o) % wide, 1)
+                wsend[p, ra, :off] = a[:, :off].astype(BF16)
+                wsend[p, ra, off:wide] = jnp.where(lane < shift, a[:, off:], b[:, :wide - off]).astype(BF16)
+                wsend[p, ra, wide:] = b[:, wide - off:].astype(BF16)
+        cs = []
+        for k in range(1, protos):
+            to = lax.rem(mp + k, protos)
+            c = remote(wsend.at[to], wgot.at[k], wssem.at[k], wrsem.at[k], {"proto": to})
+            c.start()
+            cs.append(c)
+        return cs
+
+    order = [groups // 2] + [k for k in range(1, groups) if k != groups // 2]
+    sent = {order[0]: bucket(order[0])}
+    wcopies = spread_protos()
+    for k in order[1:]:
+        sent[k] = bucket(k)
+    bucket(0)
+
+    keep = lax.broadcasted_iota(jnp.int32, (cols // 2, wide), 1) < fw
+    for k in range(protos):
+        if k:
+            wcopies[k - 1].wait()
+        src = wsend.at[mp] if k == 0 else wgot.at[k]
+        w_ref[k, :cols // 2, :] = jnp.where(keep, src[:, :wide].astype(F32), 0.0).astype(BF16)
+        b = pltpu.roll(src[:, off:].astype(F32), wide - shift, 1)
+        w_ref[k, cols // 2:, :] = jnp.where(keep, b, 0.0).astype(BF16)
 
     chunk = 512
     step = 256
     per = step // fine
-
-    def score(to, c):
-        lanes = pl.ds(pl.multiple_of(c * chunk, chunk), chunk)
-        rows = r_ref[lanes, :]
-        slots = jnp.broadcast_to(slot_ref[:1, lanes], (fine, chunk))
-        acc = jnp.zeros((fine, chunk), F32)
-        for j in range(cols // step):
-            s = lax.dot_general(w_ref[to, pl.ds(j * step, step), :], rows, NT, preferred_element_type=F32)
-            for i in range(per):
-                acc = jnp.where(slots == j * per + i + 1, s[i * fine:(i + 1) * fine], acc)
-        return lanes, acc
-
-    copies = []
-    for k in list(range(1, protos)) + [0]:
-        to = lax.rem(mp + k, protos)
-
-        @pl.loop(0, total // chunk)
+    width_m = member.shape[0]
+    cl = lax.broadcasted_iota(jnp.int32, (width_m, cap), 0) + 1
+
+    def lanes_of(k):
+        src = lax.rem(me - k + groups, groups)
+        return src, pl.ds(pl.multiple_of(src * cap, cap), cap)
+
+    def score(k):
+        src, lanes = lanes_of(k)
+        if k:
+            sent[k].wait()
+        base = src * cap
+        r_ref[pl.ds(pl.multiple_of(base, half), half), :] = got[src, :half, :wide]
+        b = got[src, :half, off:].astype(F32)
+        r_ref[pl.ds(pl.multiple_of(base + half, half), half), :] = pltpu.roll(b, wide - shift, 1).astype(BF16)
+        codes = got[src, pl.ds(half, EXTRA), :tile].astype(F32)
+        slots = jnp.concatenate([codes[u:u + 1, :] for u in range(cap // tile)], axis=1)
+        slots = jnp.broadcast_to(slots, (8, cap)).astype(jnp.int32)
+        slot_ref[:, lanes] = slots
+        member[:, lanes] = jnp.where(slots[:1] == cl, 1.0, 0.0).astype(BF16)
+
+        @pl.loop(0, cap // chunk)
         def _(c):
-            lanes, acc = score(to, c)
-            part[k, :, lanes] = acc
-
-        if k:
-            c = remote(part.at[k], prec.at[k], psem.at[k], prsem.at[k], {"proto": to})
+            at = pl.ds(pl.multiple_of(base + c * chunk, chunk), chunk)
+            x = r_ref[at, :]
+            sl = slot_ref[:, at]
+            acc = [[jnp.zeros((8, chunk), F32) for _ in range(fine // 8)] for _ in range(protos)]
+            for j in range(cols // step):
+                for p in range(protos):
+                    s = lax.dot_general(w_ref[p, j * step:(j + 1) * step, :], x, NT, preferred_element_type=F32)
+                    for i in range(per):
+                        hit = sl == j * per + i + 1
+                        for h in range(fine // 8):
+                            z = i * fine + h * 8
+                            acc[p][h] = jnp.where(hit, s[z:z + 8], acc[p][h])
+            for p in range(protos):
+                part[p, :, at] = jnp.concatenate(acc[p], axis=0)
+
+        cs = []
+        for p in range(1, protos):
+            to = lax.rem(mp - p + protos, protos)
+            c = remote(part.at[p, :, lanes], prec.at[p, :, lanes], psem.at[k, p], prsem.at[k, p], {"proto": to})
             c.start()
-            copies.append(c)
-    for c in copies:
-        c.wait()
-    live = slot_ref[:1, :] > 0
-    s = part[0]
-    for k in range(1, protos):
-        s = s + prec[k]
-    kern = jnp.where(live, jnp.exp(s * scale), 0.0).astype(BF16)
-    kall[mp] = kern
-    copies = []
-    for k in range(1, protos):
-        to = lax.rem(mp + k, protos)
-        c = remote(kall.at[mp], kall.at[mp], ksem.at[k], krsem.at[k], {"proto": to})
-        c.start()
-        copies.append(c)
-    width_m = member.shape[0]
-    cl = lax.broadcasted_iota(jnp.int32, (width_m, chunk), 0) + 1
-
-    @pl.loop(0, total // chunk)
-    def _(c):
-        lanes = pl.ds(pl.multiple_of(c * chunk, chunk), chunk)
-        member[:, lanes] = jnp.where(slot_ref[:1, lanes] == cl, 1.0, 0.0).astype(BF16)
-
-    for c in copies:
-        c.wait()
+            cs.append(c)
+        return cs
+
+    def finish(k, cs):
+        _, lanes = lanes_of(k)
+        for c in cs:
+            c.wait()
+        s = part[0, :, lanes]
+        for p in range(1, protos):
+            s = s + prec[p, :, lanes]
+        live = jnp.broadcast_to(slot_ref[:1, lanes], s.shape) > 0
+        kall[mp, :, lanes] = jnp.where(live, jnp.exp(s * scale), 0.0).astype(BF16)
+        out = []
+        for p in range(1, protos):
+            to = lax.rem(mp + p, protos)
+            c = remote(kall.at[mp, :, lanes], kall.at[mp, :, lanes], ksem.at[k, p], krsem.at[k, p], {"proto": to})
+            c.start()
+            out.append(c)
+        return out
+
+    pending, last = [], None
+    for k in [0] + order:
+        now = (k, score(k))
+        if last is not None:
+            pending += finish(*last)
+        last = now
+    pending += finish(*last)
 
     def exchange(n, value):
         xs[n] = value
@@ -181,7 +216,7 @@
         return jnp.concatenate([v, jnp.zeros((8, width_m), F32)], axis=0)
 
     nch = total // chunk
-    livef = live.astype(F32)
+    livef = (slot_ref[:1, :] > 0).astype(F32)
 
     def piece(c):
         return slice(c * chunk, (c + 1) * chunk)
@@ -192,6 +227,8 @@
     weights = [livef[:, piece(c)] for c in range(nch)]
     counts = lax.dot_general(jnp.broadcast_to(livef, (16, total)).astype(BF16), member[...], NT,
                              preferred_element_type=F32)[:8]
+    for c in pending:
+        c.wait()
     for n in range(ITERS):
         col = jnp.zeros((FPC, width_m), F32)
         for c in range(nch):
@@ -255,17 +292,19 @@
     block = 256
     per = block // fine
     chunk = 1024
+    slotf = slot_ref[:1, :].astype(F32)
     lane = lax.broadcasted_iota(jnp.int32, (block, off), 1)
 
-    def moment(to, first):
+    def moment(to, first_cluster):
+        first = lax.convert_element_type(first_cluster, F32)
         plan_rows = pl.ds(pl.multiple_of(to * fine, fine), fine)
         acc = jnp.zeros((block, wide), F32)
         for c in range(total // chunk):
             lanes = slice(c * chunk, (c + 1) * chunk)
-            plan = plan_ref[plan_rows, lanes].astype(F32)
-            slots = jnp.broadcast_to(slot_ref[:1, lanes], (fine, chunk)) - first
+            plan = plan_ref[plan_rows, lanes]
+            slots = (jnp.broadcast_to(slotf[:, lanes], (fine, chunk)) - first).astype(BF16)
             a = jnp.concatenate(
-                [jnp.where(slots == i + 1, plan, 0.0).astype(BF16) for i in range(per)], axis=0)
+                [jnp.where(slots == jnp.asarray(i + 1, BF16), plan, jnp.zeros((), BF16)) for i in range(per)], axis=0)
             acc = acc + jnp.dot(a, r_ref[lanes, :], preferred_element_type=F32)
         return acc
 
@@ -303,18 +342,19 @@
 
     for c in copies:
         c.wait()
-    nrow = dest_ref.shape[0]
+    nrow = dest_ref.shape[1]
     rt = 256
 
     @pl.loop(0, nrow // rt)
     def _(t):
         r = pl.ds(pl.multiple_of(t * rt, rt), rt)
-        acc = jnp.zeros((rt, fine), F32)
-        d = jnp.broadcast_to(dest_ref[r, :], (rt, cap))
+        acc = jnp.zeros((fine, rt), F32)
+        d = dest_ref[:, r]
         for g in range(groups):
-            hot = jnp.where(d == lax.broadcasted_iota(jnp.int32, (rt, cap), 1) + g * cap, 1.0, 0.0)
-            acc = acc + lax.dot_general(hot.astype(BF16), crec[g], NT, preferred_element_type=F32)
-        codes_ref[r, :] = acc * FPC
+            at = lax.broadcasted_iota(jnp.int32, (cap, rt), 0) + g * cap
+            hot = jnp.where(at == d, 1.0, 0.0).astype(BF16)
+            acc = acc + jnp.dot(crec[g], hot, preferred_element_type=F32)
+        codes_ref[:, r] = acc * FPC
 
     for c in mcopies:
         c.wait_send()
@@ -331,6 +371,12 @@
     lane2 = lax.broadcasted_iota(jnp.int32, (128, off), 1)
     eye = lax.broadcasted_iota(jnp.int32, (128, 128), 0) == lax.broadcasted_iota(jnp.int32, (128, 128), 1)
     n128 = packed // 128
+    mass_mine = jnp.concatenate([mass_ref[f_rows, :]] * (128 // fine), axis=0)
+    cl_lane = lax.broadcasted_iota(jnp.int32, (128, 128), 1) - lax.broadcasted_iota(jnp.int32, (128, 128), 0) // fine
+
+    def mass_of(t):
+        return jnp.sum(jnp.where(cl_lane == t * (128 // fine), mass_mine, 0.0), axis=1, keepdims=True)
+
     sums = []
     for t in range(n128):
         r = slice(t * 128, (t + 1) * 128)
@@ -348,7 +394,7 @@
         for h, vals in enumerate((first, second)):
             rr = slice(h * packed + t * 128, h * packed + (t + 1) * 128)
             mom = jnp.concatenate(vals, axis=1)
-            up = (proto_ref[rr, :].astype(F32) + mom) / (1.0 + mass_ref[rr, :])
+            up = (proto_ref[rr, :].astype(F32) + mom) / (1.0 + mass_of(h * n128 + t))
             new_ref[rr, :] = up
             q = jnp.sum(up * up, axis=1, keepdims=True)
             sums.append((h * n128 + t, jnp.sum(jnp.where(eye, jnp.broadcast_to(q, (128, 128)), 0.0), axis=0, keepdims=True)))
@@ -386,9 +432,6 @@
     total = groups * cap
     cols = clusters * fine
 
-    def quarter(p):
-        return (p % reps) * share + p // reps
-
     place = jnp.sum(jnp.where(labels[:, None] == jnp.arange(cluster_place.shape[0])[None, :],
                               cluster_place[None, :], 0), axis=1)
     target, slot = place // clusters, place % clusters
@@ -405,41 +448,34 @@
     xq = (mine * inv).astype(BF16)
     xa = jnp.pad(xq, ((0, 0), (0, wide - fw)))
     xb = jnp.pad(xq, ((0, 0), (wide - fw, 0)))
-    unit_p = unit(prototypes.astype(F32)).astype(BF16).reshape(cols, dim)
-    w = jnp.stack([jnp.pad(unit_p[:, quarter(p) * fw:(quarter(p) + 1) * fw], ((0, 0), (0, wide - fw)))
-                   for p in range(protos)])
     dma, sds = pltpu.SemaphoreType.DMA, jax.ShapeDtypeStruct
     params = functools.partial(pltpu.CompilerParams, has_side_effects=True, vmem_limit_bytes=60 * 2**20)
-    got, gotw = pl.pallas_call(
-        functools.partial(dispatch_kernel, groups, protos, cap, tile, width),
-        out_shape=(sds((groups, half + EXTRA, width), BF16), sds((protos, cols, wide), BF16)),
-        in_specs=[VM] * 5,
-        out_specs=(VM, VM),
-        scratch_shapes=[pltpu.VMEM((groups, half + EXTRA, width), BF16),
-                        dma((groups,)), dma((groups,)), dma((protos,)), dma((protos,)), dma],
-        compiler_params=params(collective_id=0),
-    )(dest[None, :], slot16, xa, xb, w)
     plan, mass, slots, r = pl.pallas_call(
-        functools.partial(sinkhorn_kernel, groups, protos, reps, cap, tile, 1.0 / (dim * SHARPNESS)),
+        functools.partial(sinkhorn_kernel, groups, protos, reps, cap, tile, width, fw, 1.0 / (dim * SHARPNESS)),
         out_shape=(sds((FPC, total), BF16), sds((FPC, 128), F32), sds((8, total), jnp.int32),
                    sds((total, wide), BF16)),
-        in_specs=[VM] * 2,
+        in_specs=[VM] * 5,
         out_specs=(VM,) * 4,
-        scratch_shapes=[pltpu.VMEM((protos, fine, total), F32), pltpu.VMEM((protos, fine, total), F32),
+        scratch_shapes=[pltpu.VMEM((groups, half + EXTRA, width), BF16),
+                        pltpu.VMEM((groups, half + EXTRA, width), BF16),
+                        pltpu.VMEM((protos, cols // 2, width), BF16),
+                        pltpu.VMEM((protos, cols // 2, width), BF16),
+                        pltpu.VMEM((protos, cols, wide), BF16),
+                        pltpu.VMEM((protos, fine, total), F32), pltpu.VMEM((protos, fine, total), F32),
                         pltpu.VMEM((128, total), BF16),
                         pltpu.VMEM((ITERS + 1, FPC + 8, 128), F32),
                         pltpu.VMEM((ITERS + 1, reps, FPC + 8, 128), F32),
                         pltpu.VMEM((protos, fine, total), BF16),
-                        dma((protos,)), dma((protos,)), dma((protos,)), dma((protos,)),
+                        dma((groups,)), dma((groups,)), dma((protos,)), dma((protos,)),
+                        dma((groups, protos)), dma((groups, protos)), dma((groups, protos)), dma((groups, protos)),
                         dma((ITERS + 1, reps)), dma((ITERS + 1, reps))],
-        compiler_params=params(collective_id=1),
-    )(got, gotw)
-    mass_col = lax.dynamic_slice_in_dim(mass, mp * fine, fine, 0)[:, :clusters].T.reshape(cols, 1)
+        compiler_params=params(collective_id=0),
+    )(dest[None, :], slot16, xa, xb, prototypes.reshape(cols, dim))
     hw = dim // reps
     proto_half = lax.dynamic_slice_in_dim(prototypes, mr * hw, hw, 2).reshape(cols, hw)
     new, codes = pl.pallas_call(
         functools.partial(update_kernel, groups, protos, reps, cap, fw),
-        out_shape=(sds((cols, hw), F32), sds((rows, fine), F32)),
+        out_shape=(sds((cols, hw), F32), sds((fine, rows), F32)),
         in_specs=[VM] * 6,
         out_specs=(VM, VM),
         scratch_shapes=[pltpu.VMEM((protos, cols // 2, width), BF16),
@@ -448,9 +484,9 @@
                         pltpu.VMEM((cols // 128, 128), F32), pltpu.VMEM((reps, cols // 128, 128), F32),
                         dma((groups,)), dma((groups,)), dma((protos,)), dma((reps * share,)), dma,
                         dma((reps,)), dma((reps,))],
-        compiler_params=params(collective_id=2),
-    )(plan, slots, r, mass_col, proto_half, dest[:, None])
-    return new.reshape(clusters, fine, hw), codes
+        compiler_params=params(collective_id=1),
+    )(plan, slots, r, mass, proto_half, dest[None, :])
+    return new.reshape(clusters, fine, hw), codes.T
 
 
 def solution(mesh):

time: 157 us -> 128 us (0.82)
  Pallas kernels: 129 us -> 111 us
  local copies, waits for them, and re-layouts: 12.8 us -> 7 us
  other arithmetic: 13 us -> 7.55 us
    pallas_call x1 -> x0, Pallas kernels: 42.1 us -> none  [body(): pl.pallas_call(functools.partial(dispatch_kernel, groups, protos, cap, ti...]
    pallas_call x1, Pallas kernels: 45.7 us -> 74.4 us  [body(): pl.pallas_call(functools.partial(sinkhorn_kernel, groups, protos, reps, c...]
    pallas_call x1, Pallas kernels: 41.3 us -> 37.1 us  [body(): pl.pallas_call(functools.partial(update_kernel, groups, protos, reps, cap...]
    select_n x2 -> x1, other arithmetic: 3.58 us -> 0.64 us  [body(): dest = jnp.where(live, target * cap + position, -1).astype(jnp.int32)]
    another operation x4 -> x2, other arithmetic: 3.14 us -> 1.34 us  [the longest x2 1.8 us: body(): jnp.stack([jnp.pad(unit_p[:, quarter(p) * fw:(quarter(p) + 1) * fw], ((0,...]
    reduce_sum x2 -> x0, local copies, waits for them, and re-layouts: 1.71 us -> none  [the longest x1 1.35 us: body(): jnp.sum(jnp.where(labels[:, None] == jnp.arange(cluster_place.shape[0])[N...]
where the time goes in v2:
time: 128 us
  Pallas kernels  111 us (87%)
  other arithmetic  7.55 us (6%)
  local copies, waits for them, and re-layouts  7 us (5%)
  between operations  1.55 us (1%)
    pallas_call x1, Pallas kernels, body(): pl.pallas_call(functools.partial(sinkhorn_kernel, groups, protos, reps, c...  74.4 us
    pallas_call x1, Pallas kernels, body(): pl.pallas_call(functools.partial(update_kernel, groups, protos, reps, cap...  37.1 us
    unnamed x10, local copies, waits for them, and re-layouts  3.37 us
    reduce_sum x1, other arithmetic, body(): inv = lax.rsqrt(jnp.mean(rows_f * rows_f, axis=-1, keepdims=True) + 1e-06)  2.57 us

profile of v2, /device:TPU:0, one launch (start us, length us, event | category | flops | bytes accessed | tf_op | source)
XLA Modules:
  0.0 127.5 jit_solution(9276365823361467286)
XLA Ops:
  0.6 2.6 %multiply_reduce_fusion = f32[2048]{0:T(1024)S(1)} fusion(bf16[2048,768]{1,0:T(8,128)(2,1)} %param.5), kind=kLoop, calls=%fused_computation | loop fusion | flops 4716544 | bytes 3153920 | tf_op jit(solution)/shard_map/reduce_sum | solution.py:445
  3.2 2.1 %multiply_convert_fusion = bf16[2048,192]{1,0:T(8,128)(2,1)S(1)} fusion(f32[2048]{0:T(1024)S(1)} %add_rsqrt_fusion, bf16[2048,768]{1,0:T(8,128)(2,1)} %param.5, s32[]{:T(128)S(6)} %select_n.69), kind=kLoop, calls=%fused_computation.1 | loop fusion | flops 1179648 | bytes 1581060 | tf_op jit(solution)/shard_map/convert_element_type | solution.py:448
  5.3 0.0 copy-start.2
  5.3 0.0 copy-start.3
  5.3 1.8 %fusion.12 = (bf16[2048,256]{1,0:T(8,128)(2,1)}, bf16[2048,256]{1,0:T(8,128)(2,1)}) fusion(bf16[2048,192]{1,0:T(8,128)(2,1)S(1)} %multiply_convert_fusion), kind=kLoop, calls=%fused_computation.42 | loop fusion | bytes 2883584 | tf_op jit(solution)/shard_map/jit(_pad)/pad | solution.py:450
  7.2 0.0 copy-done.2
  7.2 0.0 copy-done.3
  7.2 0.7 select_reduce_fusion
  7.9 0.0 copy-start
  8.7 1.2 reduce-window.6
  9.9 0.2 slice_reduce_fusion
  10.1 0.2 reduce-window.9
  10.3 0.1 add_bitcast_fusion
  10.5 0.6 compare_select_fusion.dest_ref
  11.1 0.6 broadcast_in_dim.23.slot_in_ref
  11.7 74.4 %shard_map.68 = (bf16[64,4096]{1,0:T(8,128)(2,1)}, f32[64,128]{1,0:T(8,128)}, s32[8,4096]{1,0:T(8,128)}, bf16[4096,256]{1,0:T(8,128)(2,1)}) custom-call(s32[1,2048]{1,0:T(1,128)} %compare_select_fusion.dest_ref, bf16[16,2048]{1,0:T(8,128)(2,1)} %broadcast_in_dim.23.slot_in_ref, bf16[2048,256]{1,0:T(8,128)(2,1)} %get-tuple-element.15.xa_ref, ...), custom_call_target="tpu_custom_call" | custom-call | tf_op jit(solution)/shard_map/pallas_call | solution.py:453
  86.1 0.0 copy-done
  86.1 1.0 constant_dynamic-slice_fusion
  87.1 37.1 %shard_map.69 = (f32[1024,384]{1,0:T(8,128)}, f32[16,2048]{1,0:T(8,128)}) custom-call(bf16[64,4096]{1,0:T(8,128)(2,1)} %get-tuple-element.8.plan_ref, s32[8,4096]{1,0:T(8,128)} %get-tuple-element.9.slot_ref, bf16[4096,256]{1,0:T(8,128)(2,1)} %get-tuple-element.10.r_ref, f32[64,128]{1,0:T(8,128)} %get-tuple-element.11.mass_ref, bf16[1024,384]{1,0:T(8,128)(2,1)} %bitcast.42, ...), custom_call_target="tpu_custom_call" | custom-call | tf_op jit(solution)/shard_map/pallas_call | solution.py:476
  124.2 0.0 copy-start.1
  124.2 2.7 %copy.12 = f32[64,16,384]{2,1,0:T(8,128)} copy(f32[64,16,384]{2,1,0:T(8,128)} %bitcast.43) | data formatting | bytes 3145728
  126.9 0.0 copy-done.1
  126.9 0.7 copy.13
  (7 shorter events, 0.1 us)
Async XLA Ops:
  5.3 1.8 %copy-start.2 = (s32[2048]{0:T(1024)S(1)}, s32[2048]{0:T(1024)}, u32[]{:S(2)}) copy-start(s32[2048]{0:T(1024)} %param.6) | copy-start | bytes 24580
  5.3 1.8 %copy-start.3 = (s32[256]{0:T(256)S(1)}, s32[256]{0:T(256)}, u32[]{:S(2)}) copy-start(s32[256]{0:T(256)} %param.7) | copy-start | bytes 3076
  7.9 78.2 %copy-start = (bf16[64,16,768]{2,1,0:T(8,128)(2,1)S(1)}, bf16[64,16,768]{2,1,0:T(8,128)(2,1)}, u32[]{:S(2)}) copy-start(bf16[64,16,768]{2,1,0:T(8,128)(2,1)} %param.9) | copy-start | bytes 4718596
  124.2 2.7 %copy-start.1 = (f32[16,2048]{1,0:T(8,128)S(1)}, f32[16,2048]{1,0:T(8,128)}, u32[]{:S(2)}) copy-start(f32[16,2048]{1,0:T(8,128)} %get-tuple-element.13) | copy-start | bytes 393220

commit v3 on v2

--- a/solution.py
+++ b/solution.py
@@ -40,7 +40,7 @@
 
 
 def sinkhorn_kernel(groups, protos, reps, cap, tile, width, fw, scale,
-                    dest_ref, slot_in_ref, xa_ref, xb_ref, proto_ref,
+                    dest_ref, slot_in_ref, xa_ref, proto_ref,
                     plan_ref, mass_ref, slot_ref, r_ref,
                     got, send, wsend, wgot, w_ref, part, prec, member, xs, xr, kall,
                     ssem, rsem, wssem, wrsem, psem, prsem, ksem, krsem, xsem, xrsem):
@@ -66,7 +66,7 @@
             oa = jnp.where(at == dest_ref[...], 1.0, 0.0).astype(BF16)
             ob = jnp.where(at + half == dest_ref[...], 1.0, 0.0).astype(BF16)
             a = jnp.dot(oa, xa_ref[...], preferred_element_type=F32)
-            b = jnp.dot(ob, xb_ref[...], preferred_element_type=F32)
+            b = pltpu.roll(jnp.dot(ob, xa_ref[...], preferred_element_type=F32), shift, 1)
             sa = lax.dot_general(slot_in_ref[...], oa, NT, preferred_element_type=F32)
             sb = lax.dot_general(slot_in_ref[...], ob, NT, preferred_element_type=F32)
             codes = jnp.where(row16 == t, sa, codes)
@@ -255,12 +255,12 @@
                 low = (ks * weights[c]).astype(BF16)
                 plan_ref[:, piece(c)] = low
                 mass = mass + lax.dot_general(low, m, NT, preferred_element_type=F32)
-    mass_ref[...] = exchange(ITERS, pad8(mass))[:FPC]
+    mass_ref[...] = mass
 
 
 def update_kernel(groups, protos, reps, cap, fw, plan_ref, slot_ref, r_ref, mass_ref, proto_ref, dest_ref,
                   new_ref, codes_ref, send, mrec, crec, ss, ssr,
-                  csem, crsem, msem, mrsem, lsem, ssem, ssrsem):
+                  csem, crsem, msem, mrsem, lsem, ssem, ssrsem, mx, mxsem, mxrsem):
     mg, mp, mr = lax.axis_index("group"), lax.axis_index("proto"), lax.axis_index("rep")
     total = groups * cap
     fine = FPC // protos
@@ -286,6 +286,11 @@
                    csem.at[k], crsem.at[k], {"group": to})
         c.start()
         copies.append(c)
+    mass_copies = []
+    for k in range(1, reps):
+        c = remote(mass_ref, mx.at[k], mxsem.at[k], mxrsem.at[k], {"rep": lax.rem(mr + k, reps)})
+        c.start()
+        mass_copies.append(c)
     crec_own = plan_ref[f_rows, pl.ds(pl.multiple_of(mg * cap, cap), cap)]
     crec[mg] = crec_own
 
@@ -371,7 +376,13 @@
     lane2 = lax.broadcasted_iota(jnp.int32, (128, off), 1)
     eye = lax.broadcasted_iota(jnp.int32, (128, 128), 0) == lax.broadcasted_iota(jnp.int32, (128, 128), 1)
     n128 = packed // 128
-    mass_mine = jnp.concatenate([mass_ref[f_rows, :]] * (128 // fine), axis=0)
+    hw = new_ref.shape[1]
+    half_lanes = pl.ds(pl.multiple_of(mr * hw, 128), hw)
+    mass_f = mass_ref[f_rows, :]
+    for k in range(1, reps):
+        mass_copies[k - 1].wait()
+        mass_f = mass_f + mx[k, f_rows, :]
+    mass_mine = jnp.concatenate([mass_f] * (128 // fine), axis=0)
     cl_lane = lax.broadcasted_iota(jnp.int32, (128, 128), 1) - lax.broadcasted_iota(jnp.int32, (128, 128), 0) // fine
 
     def mass_of(t):
@@ -394,7 +405,7 @@
         for h, vals in enumerate((first, second)):
             rr = slice(h * packed + t * 128, h * packed + (t + 1) * 128)
             mom = jnp.concatenate(vals, axis=1)
-            up = (proto_ref[rr, :].astype(F32) + mom) / (1.0 + mass_of(h * n128 + t))
+            up = (proto_ref[rr, half_lanes].astype(F32) + mom) / (1.0 + mass_of(h * n128 + t))
             new_ref[rr, :] = up
             q = jnp.sum(up * up, axis=1, keepdims=True)
             sums.append((h * n128 + t, jnp.sum(jnp.where(eye, jnp.broadcast_to(q, (128, 128)), 0.0), axis=0, keepdims=True)))
@@ -447,14 +458,13 @@
     mine = lax.dynamic_slice_in_dim(embeddings, q * fw, fw, 1).astype(F32)
     xq = (mine * inv).astype(BF16)
     xa = jnp.pad(xq, ((0, 0), (0, wide - fw)))
-    xb = jnp.pad(xq, ((0, 0), (wide - fw, 0)))
     dma, sds = pltpu.SemaphoreType.DMA, jax.ShapeDtypeStruct
     params = functools.partial(pltpu.CompilerParams, has_side_effects=True, vmem_limit_bytes=60 * 2**20)
     plan, mass, slots, r = pl.pallas_call(
         functools.partial(sinkhorn_kernel, groups, protos, reps, cap, tile, width, fw, 1.0 / (dim * SHARPNESS)),
         out_shape=(sds((FPC, total), BF16), sds((FPC, 128), F32), sds((8, total), jnp.int32),
                    sds((total, wide), BF16)),
-        in_specs=[VM] * 5,
+        in_specs=[VM] * 4,
         out_specs=(VM,) * 4,
         scratch_shapes=[pltpu.VMEM((groups, half + EXTRA, width), BF16),
                         pltpu.VMEM((groups, half + EXTRA, width), BF16),
@@ -463,16 +473,15 @@
                         pltpu.VMEM((protos, cols, wide), BF16),
                         pltpu.VMEM((protos, fine, total), F32), pltpu.VMEM((protos, fine, total), F32),
                         pltpu.VMEM((128, total), BF16),
-                        pltpu.VMEM((ITERS + 1, FPC + 8, 128), F32),
-                        pltpu.VMEM((ITERS + 1, reps, FPC + 8, 128), F32),
+                        pltpu.VMEM((ITERS, FPC + 8, 128), F32),
+                        pltpu.VMEM((ITERS, reps, FPC + 8, 128), F32),
                         pltpu.VMEM((protos, fine, total), BF16),
                         dma((groups,)), dma((groups,)), dma((protos,)), dma((protos,)),
                         dma((groups, protos)), dma((groups, protos)), dma((groups, protos)), dma((groups, protos)),
-                        dma((ITERS + 1, reps)), dma((ITERS + 1, reps))],
+                        dma((ITERS, reps)), dma((ITERS, reps))],
         compiler_params=params(collective_id=0),
-    )(dest[None, :], slot16, xa, xb, prototypes.reshape(cols, dim))
+    )(dest[None, :], slot16, xa, prototypes.reshape(cols, dim))
     hw = dim // reps
-    proto_half = lax.dynamic_slice_in_dim(prototypes, mr * hw, hw, 2).reshape(cols, hw)
     new, codes = pl.pallas_call(
         functools.partial(update_kernel, groups, protos, reps, cap, fw),
         out_shape=(sds((cols, hw), F32), sds((fine, rows), F32)),
@@ -483,9 +492,10 @@
                         pltpu.VMEM((groups, fine, cap), BF16),
                         pltpu.VMEM((cols // 128, 128), F32), pltpu.VMEM((reps, cols // 128, 128), F32),
                         dma((groups,)), dma((groups,)), dma((protos,)), dma((reps * share,)), dma,
-                        dma((reps,)), dma((reps,))],
+                        dma((reps,)), dma((reps,)),
+                        pltpu.VMEM((reps, FPC, 128), F32), dma((reps,)), dma((reps,))],
         compiler_params=params(collective_id=1),
-    )(plan, slots, r, mass, proto_half, dest[None, :])
+    )(plan, slots, r, mass, prototypes.reshape(cols, dim), dest[None, :])
     return new.reshape(clusters, fine, hw), codes.T
 
 

time: 128 us -> 122 us (0.953)
  Pallas kernels: 111 us -> 107 us
  local copies, waits for them, and re-layouts: 7 us -> 5.34 us
    pallas_call x1, Pallas kernels: 74.4 us -> 70.7 us  [body(): pl.pallas_call(functools.partial(sinkhorn_kernel, groups, protos, reps, c...]
    unnamed x10 -> x4, local copies, waits for them, and re-layouts: 3.37 us -> 3.35 us
where the time goes in v3:
time: 122 us
  Pallas kernels  107 us (88%)
  other arithmetic  8.26 us (7%)
  local copies, waits for them, and re-layouts  5.34 us (4%)
  between operations  1.39 us (1%)
    pallas_call x1, Pallas kernels, body(): pl.pallas_call(functools.partial(sinkhorn_kernel, groups, protos, reps, c...  70.7 us
    pallas_call x1, Pallas kernels, body(): pl.pallas_call(functools.partial(update_kernel, groups, protos, reps, cap...  36.2 us
    unnamed x4, local copies, waits for them, and re-layouts  3.35 us
    reduce_sum x1, other arithmetic, body(): inv = lax.rsqrt(jnp.mean(rows_f * rows_f, axis=-1, keepdims=True) + 1e-06)  2.57 us

profile of v3, /device:TPU:0, one launch (start us, length us, event | category | flops | bytes accessed | tf_op | source)
XLA Modules:
  0.0 121.9 jit_solution(8895489934970114473)
XLA Ops:
  1.3 1.4 %select_reduce_fusion = s32[2048]{0:T(1024)S(1)} fusion(s32[256]{0:T(256)} %param.7, s32[2048]{0:T(1024)} %param.6), kind=kLoop, calls=%fused_computation.2 | loop fusion | flops 1570816 | bytes 17408 | tf_op jit(solution)/shard_map/reduce_sum | solution.py:446
  2.8 2.6 %multiply_reduce_fusion = f32[2048]{0:T(1024)S(1)} fusion(bf16[2048,768]{1,0:T(8,128)(2,1)} %param.5), kind=kLoop, calls=%fused_computation | loop fusion | flops 4716544 | bytes 3153920 | tf_op jit(solution)/shard_map/reduce_sum | solution.py:456
  5.4 1.2 reduce-window.6
  6.6 0.2 slice_reduce_fusion
  6.8 0.2 reduce-window.9
  7.0 0.1 add_bitcast_fusion
  7.1 0.6 compare_select_fusion.dest_ref
  7.8 0.6 broadcast_in_dim.23.slot_in_ref
  8.4 2.1 %multiply_convert_fusion = bf16[2048,192]{1,0:T(8,128)(2,1)S(1)} fusion(f32[2048]{0:T(1024)S(1)} %add_rsqrt_fusion, bf16[2048,768]{1,0:T(8,128)(2,1)} %param.5, s32[]{:T(128)S(6)} %select_n.66), kind=kLoop, calls=%fused_computation.1 | loop fusion | flops 1179648 | bytes 1581060 | tf_op jit(solution)/shard_map/convert_element_type | solution.py:459
  10.5 1.1 pad.4.xa_ref
  11.6 70.7 %shard_map.68 = (bf16[64,4096]{1,0:T(8,128)(2,1)}, f32[64,128]{1,0:T(8,128)}, s32[8,4096]{1,0:T(8,128)}, bf16[4096,256]{1,0:T(8,128)(2,1)}) custom-call(s32[1,2048]{1,0:T(1,128)} %compare_select_fusion.dest_ref, bf16[16,2048]{1,0:T(8,128)(2,1)} %broadcast_in_dim.23.slot_in_ref, bf16[2048,256]{1,0:T(8,128)(2,1)} %pad.4.xa_ref, bf16[1024,768]{1,0:T(8,128)(2,1)} %bitcast.40), custom_call_target="tpu_custom_call" | custom-call | tf_op jit(solution)/shard_map/pallas_call | solution.py:463
  82.3 36.2 %shard_map.69 = (f32[1024,384]{1,0:T(8,128)}, f32[16,2048]{1,0:T(8,128)}) custom-call(bf16[64,4096]{1,0:T(8,128)(2,1)} %get-tuple-element.8.plan_ref, s32[8,4096]{1,0:T(8,128)} %get-tuple-element.9.slot_ref, bf16[4096,256]{1,0:T(8,128)(2,1)} %get-tuple-element.10.r_ref, f32[64,128]{1,0:T(8,128)} %get-tuple-element.11.mass_ref, bf16[1024,768]{1,0:T(8,128)(2,1)} %bitcast.41, ...), custom_call_target="tpu_custom_call" | custom-call | tf_op jit(solution)/shard_map/pallas_call | solution.py:485
  118.6 0.0 copy-start
  118.6 2.7 %copy.12 = f32[64,16,384]{2,1,0:T(8,128)} copy(f32[64,16,384]{2,1,0:T(8,128)} %bitcast.42) | data formatting | bytes 3145728
  121.3 0.0 copy-done
  121.3 0.7 copy.13
  (7 shorter events, 0.1 us)
Async XLA Ops:
  118.6 2.7 %copy-start = (f32[16,2048]{1,0:T(8,128)S(1)}, f32[16,2048]{1,0:T(8,128)}, u32[]{:S(2)}) copy-start(f32[16,2048]{1,0:T(8,128)} %get-tuple-element.13) | copy-start | bytes 393220
